TPU v7x, 256 devices: a whole 4x4x8 slice. The times are simulated.
256 devices in a mesh: doc: 64 (over z, y, core), tp: 4 (over x).
Axes of the slice: x: 4, y: 4, z: 8, core: 2. Of those that a mesh axis runs over, the one named last changes fastest.
Arguments:
- storage: bfloat16 [32768, 3584], P('doc', 'tp'), may hold values from -40 to 40
- row_doc: int32 [32768], P('doc'), may hold values from -1 to 63, as said below
- row_pos: int32 [32768], P('doc'), may hold values from -1 to 511, as said below
- doc_len: int32 [64], replicated, may hold values from 64 to 512, as said below
- partner: int32 [64], replicated, may hold values from 0 to 63, as said below
- norm_gain: bfloat16 [3584], replicated, may hold values from 0.25 to 1.75
- qkv_weight: bfloat16 [3584, 4608], P('doc', 'tp'), may hold values from -0.09375 to 0.09375
- qkv_bias: bfloat16 [4608], P('tp'), may hold values from -24 to 24
Outputs:
- attention: bfloat16 [65536, 3584], P('doc', 'tp')
Inputs may be any that keep to these rules, and one draw needn't show every extreme that they name: `row_doc`: the rows 0 to doc_len[d] - 1 of each document d are stored exactly once over all devices, one to a slot; -1 marks an empty slot. One device stores at most 8 rows of any one document, and exactly 8 rows of a document of 512 tokens. `row_pos`: -1 for an empty slot. `doc_len`: some document has 512 tokens and some has 64. partner[partner[d]] = d and partner[d] != d.
All inputs are finite; a program needn't handle non-finite values.
Results may differ from a plain program's by a relative error of at most 0.008.
The roundings to bfloat16 on the way count: a program that leaves them out, or rounds other values in their place, can miss the bound.
Values may be sent and summed in bfloat16 or wider, within the bound.
A program may use at most 64 MiB of HBM per device.

v0:
```python
import jax
import jax.numpy as jnp
from jax import lax
from jax.sharding import PartitionSpec as P

HEADS = 28
KVH = 4
HD = 128
HALF = 512
ROPE_BASE = 1000000.0
EPSILON = 1e-06
BLOCK_ROWS = 512


def from_partner(value, axis, stride):
    mask = 2**stride
    pairs = [(source, source ^ mask) for source in range(lax.axis_size(axis))]
    return lax.ppermute(value, axis, pairs)


def pairing(partner):
    doc_ids = jnp.arange(partner.shape[0], dtype=jnp.int32)
    first_flag = (doc_ids < partner).astype(jnp.int32)
    before = jnp.cumsum(first_flag) - first_flag
    low_doc = jnp.minimum(doc_ids, partner)
    pick_mask = (low_doc[:, None] == doc_ids[None, :]).astype(jnp.int32)
    pair_index = jnp.sum(pick_mask * before[None, :], axis=1)
    scorer = 2 * pair_index + 1 - first_flag
    match_mask = (scorer[None, :] == doc_ids[:, None]).astype(jnp.int32)
    own_doc = jnp.sum(match_mask * doc_ids[None, :], axis=1)
    return (scorer, own_doc)


def rope_tables(length, head_dim):
    half_dim = head_dim // 2
    freq_ids = jnp.arange(half_dim, dtype=jnp.float32)
    inv_freq = jnp.exp(-(2.0 * freq_ids / head_dim) * jnp.log(jnp.float32(ROPE_BASE)))
    angles = jnp.arange(length, dtype=jnp.float32)[:, None] * inv_freq[None, :]
    cosine = jnp.concatenate([jnp.cos(angles), jnp.cos(angles)], axis=1)
    sine_table = jnp.concatenate([jnp.sin(angles), jnp.sin(angles)], axis=1)
    return (cosine, sine_table)


def rotate(heads, cosine, sine_table):
    widened = heads.astype(jnp.float32)
    half_dim = widened.shape[-1] // 2
    turned = jnp.concatenate([-widened[..., half_dim:], widened[..., :half_dim]], axis=-1)
    return (widened * cosine[:, None, :] + turned * sine_table[:, None, :]).astype(jnp.bfloat16)


def rms_norm(row_values, norm_gain):
    widened = row_values.astype(jnp.float32)
    inv_rms = lax.rsqrt(jnp.mean(widened * widened, axis=-1, keepdims=True) + EPSILON)
    return (widened * inv_rms * norm_gain.astype(jnp.float32)).astype(jnp.bfloat16)


def place_rows(values, dest_index, length):
    blank_rows = jnp.zeros((length,) + values.shape[1:], values.dtype)
    return blank_rows.at[dest_index].set(values, mode="drop")


def assemble(first_part, second_part, first_len):
    padded = jnp.concatenate([first_part, jnp.zeros_like(second_part)], axis=0)
    return lax.dynamic_update_slice(padded, second_part, (first_len, jnp.int32(0)))


def attention(projected, total_len, q_heads, kv_heads, head_dim):
    length = projected.shape[0]
    cosine, sine_table = rope_tables(length, head_dim)
    queries = rotate(
        projected[:, : q_heads * head_dim].reshape(length, q_heads, head_dim), cosine, sine_table
    )
    key_heads = rotate(
        projected[:, q_heads * head_dim : (q_heads + kv_heads) * head_dim].reshape(
            length, kv_heads, head_dim
        ),
        cosine,
        sine_table,
    )
    value_heads = projected[:, (q_heads + kv_heads) * head_dim :].reshape(
        length, kv_heads, head_dim
    )
    grouped = queries.reshape(length, kv_heads, q_heads // kv_heads, head_dim)
    block_length = min(BLOCK_ROWS, length)
    root_dim = jnp.sqrt(jnp.float32(head_dim))
    pieces = []
    for row_start in range(0, length, block_length):
        row_stop = row_start + block_length
        scores = (
            jnp.einsum(
                "qkgd,skd->kgqs",
                grouped[row_start:row_stop],
                key_heads[:row_stop],
                preferred_element_type=jnp.float32,
            )
            / root_dim
        )
        row_ids = jnp.arange(row_start, row_stop, dtype=jnp.int32)[:, None]
        col_ids = jnp.arange(row_stop, dtype=jnp.int32)[None, :]
        allowed = (col_ids <= row_ids) & (col_ids < total_len)
        scores = jnp.where(allowed, scores, -jnp.inf)
        largest = jnp.max(scores, axis=-1, keepdims=True)
        exponent = jnp.exp(scores - largest)
        probabilities = (exponent / jnp.sum(exponent, axis=-1, keepdims=True)).astype(jnp.bfloat16)
        mixture = jnp.einsum(
            "kgqs,skd->qkgd",
            probabilities,
            value_heads[:row_stop],
            preferred_element_type=jnp.float32,
        )
        live_rows = (jnp.arange(row_start, row_stop, dtype=jnp.int32) < total_len)[
            :, None, None, None
        ]
        mixture = jnp.where(live_rows, mixture, 0.0)
        pieces.append(mixture.astype(jnp.bfloat16).reshape(block_length, q_heads * head_dim))
    return jnp.concatenate(pieces, axis=0)


def shards(storage, row_doc, row_pos, doc_len, partner, norm_gain, qkv_weight, qkv_bias):
    doc_count = lax.axis_size("doc")
    me_index = lax.axis_index("doc")
    half_rows = HALF
    per_dest = half_rows // doc_count
    scorer, own_doc = pairing(partner)
    doc_ids = jnp.arange(doc_count, dtype=jnp.int32)
    first_doc = jnp.sum(jnp.where(doc_ids == me_index, own_doc, 0))
    second_doc = jnp.sum(jnp.where(doc_ids == first_doc, partner, 0))
    first_len = jnp.sum(jnp.where(doc_ids == first_doc, doc_len, 0))
    second_len = jnp.sum(jnp.where(doc_ids == second_doc, doc_len, 0))
    total_len = first_len + second_len
    stored = row_doc >= 0
    dest_scorer = jnp.sum(
        jnp.where(row_doc[:, None] == doc_ids[None, :], scorer[None, :], 0), axis=1
    )
    onehot = ((dest_scorer[:, None] == doc_ids[None, :]) & stored[:, None]).astype(jnp.int32)
    dest_rank = jnp.sum(jnp.cumsum(onehot, axis=0) * onehot, axis=1) - 1
    dest_index = jnp.where(stored, dest_scorer * per_dest + dest_rank, doc_count * per_dest)
    send_rows = place_rows(storage, dest_index, doc_count * per_dest).reshape(
        doc_count, per_dest, storage.shape[1]
    )
    send_pos = (
        jnp.full((doc_count * per_dest,), half_rows, jnp.int32)
        .at[dest_index]
        .set(row_pos, mode="drop")
    )
    send_pos = send_pos.reshape(doc_count, per_dest)
    got_rows, got_pos = (
        lax.all_to_all(send_rows, "doc", split_axis=0, concat_axis=0, tiled=True),
        lax.all_to_all(send_pos, "doc", split_axis=0, concat_axis=0, tiled=True),
    )
    own_rows = place_rows(
        got_rows.reshape(doc_count * per_dest, storage.shape[1]), got_pos.reshape(-1), half_rows
    )
    q_heads = HEADS // lax.axis_size("tp")
    kv_heads = KVH // lax.axis_size("tp")
    bias_wide = qkv_bias.astype(jnp.float32)
    other_rows = from_partner(own_rows, "doc", 0)
    both_full = lax.all_gather(
        jnp.concatenate([own_rows, other_rows], axis=0), "tp", axis=1, tiled=True
    )
    normed = rms_norm(both_full, norm_gain)
    full_weight = lax.all_gather(qkv_weight, "doc", axis=0, tiled=True)
    both_sum = jnp.dot(normed, full_weight, preferred_element_type=jnp.float32)
    both_proj = (both_sum + bias_wide).astype(jnp.bfloat16)
    projected = assemble(both_proj[:half_rows], both_proj[half_rows:], first_len)
    return attention(projected, total_len, q_heads, kv_heads, HD)


def solution(mesh):
    placed = (P("doc", "tp"), P("doc"), P("doc"), P(), P(), P(), P("doc", "tp"), P("tp"))
    return jax.shard_map(
        shards, mesh=mesh, in_specs=placed, out_specs=P("doc", "tp"), check_vma=False
    )
```

profile of v0, /device:TPU:1, one launch (start us, length us, event | category | flops | bytes accessed | tf_op | source)
XLA Modules:
  0.0 322.1 jit_solution(13756107359092494782)
XLA Ops:
  11.2 1.2 reduce-window.20
  13.5 2.6 scatter_custom_fusion
  16.8 13.2 %all-to-all-start = ((s32[64,1,8]{2,1,0:T(1,128)}), s32[64,1,8]{2,1,0:T(1,128)S(1)}, u32[]{:S(2)}, u32[]{:S(2)}) async-start(s32[64,1,8]{2,1,0:T(1,128)} %bitcast.4), calls=%async_computation | async-start | bytes 65536 | tf_op jit(solution)/shard_map/all_to_all | solution.py:149
  29.9 4.3 %scatter_custom_fusion.1 = bf16[512,896]{1,0:T(8,128)(2,1)} fusion(s32[512]{0:T(512)S(1)} %compare_select_fusion.1, bf16[512,896]{1,0:T(8,128)(2,1)} %param.8, bf16[]{:T(256)} %constant.24.clone.1), kind=kCustom, calls=%fused_computation.63 | custom fusion | bytes 918016 | tf_op jit(solution)/shard_map/scatter | solution.py:59
  34.2 5.1 %all-to-all-done = s32[64,1,8]{2,1,0:T(1,128)S(1)} async-done(((s32[64,1,8]{2,1,0:T(1,128)}), s32[64,1,8]{2,1,0:T(1,128)S(1)}, u32[]{:S(2)}, u32[]{:S(2)}) %all-to-all-start) | async-done | bytes 2080 | tf_op jit(solution)/shard_map/all_to_all | solution.py:149
  39.3 5.2 %all-to-all-start.1 = ((bf16[64,8,896]{2,1,0:T(8,128)(2,1)}), bf16[64,8,896]{2,1,0:T(8,128)(2,1)S(1)}, u32[]{:S(2)}, u32[]{:S(2)}) async-start(bf16[64,8,896]{2,1,0:T(8,128)(2,1)} %bitcast.6), calls=%async_computation.1 | async-start | bytes 1835008 | tf_op jit(solution)/shard_map/all_to_all | solution.py:148
  46.0 23.8 %all-to-all-done.1 = bf16[64,8,896]{2,1,0:T(8,128)(2,1)S(1)} async-done(((bf16[64,8,896]{2,1,0:T(8,128)(2,1)}), bf16[64,8,896]{2,1,0:T(8,128)(2,1)S(1)}, u32[]{:S(2)}, u32[]{:S(2)}) %all-to-all-start.1) | async-done | bytes 917536 | tf_op jit(solution)/shard_map/all_to_all | solution.py:148
  69.8 2.9 scatter_custom_fusion.2
  72.8 1.3 collective-permute-start
  74.1 2.1 collective-permute-done
  76.2 1.4 pad_maximum_fusion
  79.1 1.2 fusion.51
  80.4 1.8 fusion.53
  85.6 1.9 fusion.38
  87.6 63.3 %all-gather.3.cloned.1.call-done = bf16[1024,3584]{1,0:T(8,128)(2,1)} async-done(((bf16[1024,896]{1,0:T(8,128)(2,1)}), bf16[1024,3584]{1,0:T(8,128)(2,1)}) %all-gather.3.cloned.1.call-update) | async-done | bytes 7340048 | tf_op jit(solution)/shard_map/all_gather | solution.py:158
  150.9 4.6 %fusion = f32[1024]{0:T(1024)S(1)} fusion(bf16[1024,3584]{1,0:T(8,128)(2,1)} %all-gather.3.cloned.1.call-done), kind=kLoop, calls=%fused_computation.5 | loop fusion | flops 11009024 | bytes 7344128 | tf_op jit(solution)/shard_map/reduce_sum | solution.py:53
  155.5 82.3 %all-gather.5.cloned.1.call-done = bf16[3584,1152]{1,0:T(8,128)(2,1)} async-done(((bf16[56,1152]{1,0:T(8,128)(2,1)}), bf16[3584,1152]{1,0:T(8,128)(2,1)}) %all-gather.5.cloned.1.call-update) | async-done | bytes 8257552 | tf_op jit(solution)/shard_map/all_gather | solution.py:162
  237.8 15.6 %broadcast_select_fusion = (bf16[1024,1152]{1,0:T(8,128)(2,1)}, bf16[1024,1152]{1,0:T(8,128)(2,1)S(1)}) fusion(pred[1024]{0:T(1024)(128)(4,1)S(1)} %copy-done.5, f32[1152]{0:T(1024)S(1)} %convert_element_type.67, bf16[3584,1152]{1,0:T(8,128)(2,1)} %all-gather.5.cloned.1.call-done, bf16[1024,3584]{1,0:T(8,128)(2,1)} %all-gather.3.cloned.1.call-done, ...), kind=kOutput, calls=%fused_computation.31 | convolution fusion | flops 8473935872 | bytes 20340224 | tf_op jit(solution)/shard_map/dot_general | solution.py:163
  253.4 6.3 %dynamic_update_slice.3 = bf16[1024,1152]{1,0:T(8,128)(2,1)} dynamic-update-slice(bf16[1024,1152]{1,0:T(8,128)(2,1)} %get-tuple-element.18, bf16[512,1152]{1,0:T(8,128)(2,1)S(1)} %slice.64, s32[]{:T(128)S(6)} %select_n.63, s32[]{:T(128)} %constant.20.clone.1) | dynamic-update-slice | bytes 2359300 | tf_op jit(solution)/shard_map/dynamic_update_slice | solution.py:64
  260.8 3.6 %slice_convert_fusion = f32[1024,896]{1,0:T(8,128)} fusion(bf16[1024,1152]{1,0:T(8,128)(2,1)} %dynamic_update_slice.3), kind=kLoop, calls=%fused_computation.34 | loop fusion | flops 917504 | bytes 5505024 | tf_op jit(solution)/shard_map/convert_element_type | solution.py:45
  264.5 5.1 %copy.47 = f32[1024,896]{0,1:T(8,128)} copy(f32[1024,896]{1,0:T(8,128)} %slice_convert_fusion) | data formatting | bytes 7340032 | tf_op jit(solution)/shard_map/convert_element_type | solution.py:45
  269.6 5.0 %copy.48 = f32[1024,7,128]{2,0,1:T(8,128)} copy(f32[1024,7,128]{0,2,1:T(8,128)} %bitcast.104) | data formatting | bytes 7340032 | tf_op jit(solution)/shard_map/convert_element_type | solution.py:45
  274.6 4.4 %slice_negate_fusion = (f32[1024,7,64]{2,0,1:T(8,128)S(1)}, f32[1024,7,64]{2,0,1:T(8,128)S(1)}) fusion(f32[1024,7,128]{2,0,1:T(8,128)} %copy.48), kind=kLoop, calls=%fused_computation.24 | loop fusion | flops 458752 | bytes 7340032 | tf_op jit(solution)/shard_map/neg | solution.py:47
  279.0 1.6 fusion.35
  282.3 1.3 fusion.12
  283.5 1.5 fusion.11
  285.1 4.0 %fusion.22 = bf16[1,128,7,512]{3,1,2,0:T(8,128)(2,1)} fusion(f32[7,512]{1,0:T(8,128)S(1)} %fusion.11, f32[7,512]{1,0:T(8,128)S(1)} %get-tuple-element.22, f32[512,512,7]{1,0,2:T(8,128)S(1)} %get-tuple-element.23, pred[512,512]{0,1:T(8,128)(4,1)S(1)} %fusion.27, pred[512]{0:T(512)(128)(4,1)S(1)} %get-tuple-element.24, bf16[1024,1152]{1,0:T(8,128)(2,1)} %dynamic_update_slice.3), kind=kOutput, calls=%fused_computation.40 | convolution fusion | flops 479854592 | bytes 8679936 | tf_op jit(solution)/shard_map/kgqs,skd->qkgd/dot_general | solution.py:105
  289.1 1.5 copy.55
  290.7 6.8 %fusion.4 = (f32[7,512]{1,0:T(8,128)S(1)}, f32[1024,512,7]{1,0,2:T(8,128)}) fusion(pred[512,1024]{0,1:T(8,128)(4,1)S(1)} %fusion.20, bf16[1024,7,128]{2,0,1:T(8,128)(2,1)S(1)} %fusion.16, bf16[1024,128]{1,0:T(8,128)(2,1)S(1)} %get-tuple-element.9), kind=kOutput, calls=%fused_computation.12 | convolution fusion | flops 950530560 | bytes 16398336 | tf_op jit(solution)/shard_map/qkgd,skd->kgqs/dot_general | solution.py:90
  297.4 8.2 %fusion.3 = f32[7,512]{1,0:T(8,128)S(1)} fusion(f32[1024,512,7]{1,0,2:T(8,128)} %get-tuple-element.21, f32[7,512]{1,0:T(8,128)S(1)} %get-tuple-element.20, pred[512,1024]{0,1:T(8,128)(4,1)S(1)} %fusion.20), kind=kLoop, calls=%fused_computation.11 | loop fusion | flops 14676480 | bytes 15233024 | tf_op jit(solution)/shard_map/reduce_sum | solution.py:104
  305.6 7.7 %fusion.21 = bf16[1,128,7,512]{3,1,2,0:T(8,128)(2,1)S(1)} fusion(f32[7,512]{1,0:T(8,128)S(1)} %fusion.3, f32[7,512]{1,0:T(8,128)S(1)} %get-tuple-element.20, f32[1024,512,7]{1,0,2:T(8,128)} %get-tuple-element.21, pred[512,1024]{0,1:T(8,128)(4,1)S(1)} %fusion.20, pred[512]{0:T(512)(128)(4,1)S(1)} %get-tuple-element.25, ...), kind=kOutput, calls=%fused_computation.38 | convolution fusion | flops 958791680 | bytes 16413184 | tf_op jit(solution)/shard_map/kgqs,skd->qkgd/dot_general | solution.py:105
  313.9 1.4 pad_maximum_fusion.1
  (53 shorter events, 13.6 us)
Async XLA Ops:
  16.8 22.5 %all-to-all-start = ((s32[64,1,8]{2,1,0:T(1,128)}), s32[64,1,8]{2,1,0:T(1,128)S(1)}, u32[]{:S(2)}, u32[]{:S(2)}) async-start(s32[64,1,8]{2,1,0:T(1,128)} %bitcast.4), calls=%async_computation | async-start | bytes 65536 | tf_op jit(solution)/shard_map/all_to_all | solution.py:149
  39.3 30.5 %all-to-all-start.1 = ((bf16[64,8,896]{2,1,0:T(8,128)(2,1)}), bf16[64,8,896]{2,1,0:T(8,128)(2,1)S(1)}, u32[]{:S(2)}, u32[]{:S(2)}) async-start(bf16[64,8,896]{2,1,0:T(8,128)(2,1)} %bitcast.6), calls=%async_computation.1 | async-start | bytes 1835008 | tf_op jit(solution)/shard_map/all_to_all | solution.py:148
  44.5 106.4 %all-gather.3.cloned.1.call-start = ((), (), s32[]{:S(2)}) async-start(), calls=%async_computation.2 | async-start | bytes 9175040 | tf_op jit(solution)/shard_map/all_gather | solution.py:158
  69.8 8.5 %copy-start.1 = (bf16[3584]{0:T(1024)(128)(2,1)S(1)}, bf16[3584]{0:T(1024)(128)(2,1)}, u32[]{:S(2)}) copy-start(bf16[3584]{0:T(1024)(128)(2,1)} %param.13) | copy-start | bytes 21508
  69.8 8.6 %copy-start.2 = (bf16[1152]{0:T(1024)(128)(2,1)S(1)}, bf16[1152]{0:T(1024)(128)(2,1)}, u32[]{:S(2)}) copy-start(bf16[1152]{0:T(1024)(128)(2,1)} %param.15) | copy-start | bytes 6916
  69.8 9.3 %copy-start.4 = (s32[64]{0:T(128)S(1)}, s32[64]{0:T(128)}, u32[]{:S(2)}) copy-start(s32[64]{0:T(128)} %param.12) | copy-start | bytes 772
  69.8 10.6 %copy-start.3 = (s32[64]{0:T(128)S(1)}, s32[64]{0:T(128)}, u32[]{:S(2)}) copy-start(s32[64]{0:T(128)} %param.11) | copy-start | bytes 772
  72.8 3.4 %collective-permute-start = (bf16[512,896]{1,0:T(8,128)(2,1)S(1)}, bf16[512,896]{1,0:T(8,128)(2,1)S(1)}, u32[]{:S(2)}, u32[]{:S(2)}) collective-permute-start(bf16[512,896]{1,0:T(8,128)(2,1)S(1)} %scatter_custom_fusion.2), channel_id=1, source_target_pairs={{0,4},{4,0},{8,12},{12,8},{16,20},{20,16},{24,28},{28,24},{32,36},... | collective-permute-start | bytes 2752520 | tf_op jit(solution)/shard_map/ppermute | solution.py:18
  77.6 160.2 %all-gather.5.cloned.1.call-start = ((), (), s32[]{:S(2)}) async-start(), calls=%async_computation.3 | async-start | bytes 8386560 | tf_op jit(solution)/shard_map/all_gather | solution.py:162
  87.6 150.2 %copy-start.5 = (pred[1024]{0:T(1024)(128)(4,1)S(1)}, pred[1024]{0:T(1024)(128)(4,1)}, u32[]{:S(2)}) copy-start(pred[1024]{0:T(1024)(128)(4,1)} %constant.16.clone.1) | copy-start | bytes 3076
  279.0 2.1 copy-start
Sparse Core Ops, SparseCore 0:
  77.7 73.1 all-gather.2
  153.6 84.1 all-gather.4
where the time goes:
time: 323 us; the launch traced here: 322 us
  waiting for transfers between devices  177 us (55%)
  other arithmetic  42.6 us (13%)
  matrix products  35.3 us (11%)
  local copies, waits for them, and re-layouts  30.7 us (10%)
  starting transfers between devices  19.9 us (6%)
  between operations  16.5 us (5%)
    all_gather x1, waiting for transfers between devices, shards(): full_weight = lax.all_gather(qkv_weight, 'doc', axis=0, tiled=True)  82.3 us
    all_gather x1, waiting for transfers between devices, shards(): lax.all_gather(jnp.concatenate([own_rows, other_rows], axis=0), 'tp', axi...  63.3 us
    all_to_all x1, waiting for transfers between devices, shards(): lax.all_to_all(send_rows, 'doc', split_axis=0, concat_axis=0, tiled=True)  23.8 us
    dot_general x1, matrix products, shards(): both_sum = jnp.dot(normed, full_weight, preferred_element_type=jnp.float32)  15.6 us
    all_to_all x1, starting transfers between devices, shards(): lax.all_to_all(send_pos, 'doc', split_axis=0, concat_axis=0, tiled=True)  13.2 us
    dot_general x2, matrix products, attention(): jnp.einsum('kgqs,skd->qkgd', probabilities, value_heads[:row_stop], prefe...  11.7 us
    convert_element_type x2, local copies, waits for them, and re-layouts, rotate(): widened = heads.astype(jnp.float32)  10.1 us
    reduce_sum x2, other arithmetic, attention(): jnp.sum(exponent, axis=-1, keepdims=True)  9.7 us
  transfers between devices with their start and end apart: 5, of which 5 were waited for; matrix products, arithmetic and copies ran while one was open for 5% of the time, Pallas kernels for 0%

commit v1 on v0

--- a/solution.py
+++ b/solution.py
@@ -155,9 +155,25 @@
     kv_heads = KVH // lax.axis_size("tp")
     bias_wide = qkv_bias.astype(jnp.float32)
     other_rows = from_partner(own_rows, "doc", 0)
-    both_full = lax.all_gather(
-        jnp.concatenate([own_rows, other_rows], axis=0), "tp", axis=1, tiled=True
-    )
+    array = jnp.concatenate([own_rows, other_rows], axis=0)
+    size, mine, extent = (lax.axis_size("tp"), lax.axis_index("tp"), array.shape[1])
+    right = [(i, (i + 1) % size) for i in range(size)]
+    downward = [(i, (i - 1) % size) for i in range(size)]
+    filled = jnp.zeros((*array.shape[:1], size * extent, *array.shape[1 + 1 :]), array.dtype)
+    filled = lax.dynamic_update_slice_in_dim(filled, array, mine * extent, axis=1)
+    from_left = from_right = array
+    half = size // 2
+    for step in range(1, half + 1):
+        from_left = lax.ppermute(from_left, "tp", right)
+        filled = lax.dynamic_update_slice_in_dim(
+            filled, from_left, (mine - step) % size * extent, axis=1
+        )
+        if step < size - half:
+            from_right = lax.ppermute(from_right, "tp", downward)
+            filled = lax.dynamic_update_slice_in_dim(
+                filled, from_right, (mine + step) % size * extent, axis=1
+            )
+    both_full = filled
     normed = rms_norm(both_full, norm_gain)
     full_weight = lax.all_gather(qkv_weight, "doc", axis=0, tiled=True)
     both_sum = jnp.dot(normed, full_weight, preferred_element_type=jnp.float32)

time: 323 us -> 255 us (0.79)
  waiting for transfers between devices: 177 us -> 99.2 us
  local copies, waits for them, and re-layouts: 30.7 us -> 40 us
  other arithmetic: 42.6 us -> 39 us
    all_gather x1, waiting for transfers between devices: 82.3 us -> 0.02 us  [shards(): full_weight = lax.all_gather(qkv_weight, 'doc', axis=0, tiled=True)]
    ppermute x0 -> x3, waiting for transfers between devices: none -> 66.5 us  [the longest x2 66.5 us: shards(): from_left = lax.ppermute(from_left, 'tp', right)]
    all_gather x1 -> x0, waiting for transfers between devices: 63.3 us -> none  [shards(): lax.all_gather(jnp.concatenate([own_rows, other_rows], axis=0), 'tp', axi...]
    dynamic_update_slice x0 -> x4, local copies, waits for them, and re-layouts: none -> 5.69 us  [the longest x2 3.59 us: shards(): lax.dynamic_update_slice_in_dim(filled, from_left, (mine - step) % size *...]
  transfers between devices with their start and end apart: 5 -> 7, of which waited for: 5 -> 5; matrix products, arithmetic and copies ran while one was open for 5% -> 13% of each run, Pallas kernels for 0% -> 0%
where the time goes in v1:
time: 255 us; the launch traced here: 253 us
  waiting for transfers between devices  99.2 us (39%)
  local copies, waits for them, and re-layouts  40 us (16%)
  other arithmetic  39 us (15%)
  matrix products  35.4 us (14%)
  starting transfers between devices  22.7 us (9%)
  between operations  17.1 us (7%)
    ppermute x2, waiting for transfers between devices, shards(): from_left = lax.ppermute(from_left, 'tp', right)  66.5 us
    all_to_all x1, waiting for transfers between devices, shards(): lax.all_to_all(send_rows, 'doc', split_axis=0, concat_axis=0, tiled=True)  24.8 us
    dot_general x1, matrix products, shards(): both_sum = jnp.dot(normed, full_weight, preferred_element_type=jnp.float32)  15.6 us
    all_to_all x1, starting transfers between devices, shards(): lax.all_to_all(send_pos, 'doc', split_axis=0, concat_axis=0, tiled=True)  13.2 us
    dot_general x2, matrix products, attention(): jnp.einsum('kgqs,skd->qkgd', probabilities, value_heads[:row_stop], prefe...  12 us
    convert_element_type x2, local copies, waits for them, and re-layouts, rotate(): widened = heads.astype(jnp.float32)  10.1 us
    reduce_sum x2, other arithmetic, attention(): jnp.sum(exponent, axis=-1, keepdims=True)  9.7 us
    dot_general x2, matrix products, attention(): jnp.einsum('qkgd,skd->kgqs', grouped[row_start:row_stop], key_heads[:row_...  7.79 us
  transfers between devices with their start and end apart: 7, of which 5 were waited for; matrix products, arithmetic and copies ran while one was open for 13% of the time, Pallas kernels for 0%

profile of v1, /device:TPU:1, one launch (start us, length us, event | category | flops | bytes accessed | tf_op | source)
XLA Modules:
  0.0 253.3 jit_solution(271130184569147530)
XLA Ops:
  14.2 2.6 %scatter_custom_fusion = s32[512]{0:T(512)S(1)} fusion(s32[512]{0:T(512)S(1)} %compare_select_fusion.1, s32[512]{0:T(512)} %param.10, s32[]{:T(128)} %constant.74.clone.1), kind=kCustom, calls=%fused_computation.98 | custom fusion | bytes 2560 | tf_op jit(solution)/shard_map/scatter | solution.py:144
  17.5 13.2 %all-to-all-start = ((s32[64,1,8]{2,1,0:T(1,128)}), s32[64,1,8]{2,1,0:T(1,128)S(1)}, u32[]{:S(2)}, u32[]{:S(2)}) async-start(s32[64,1,8]{2,1,0:T(1,128)} %bitcast.4), calls=%async_computation | async-start | bytes 65536 | tf_op jit(solution)/shard_map/all_to_all | solution.py:149
  30.7 4.3 %scatter_custom_fusion.1 = bf16[512,896]{1,0:T(8,128)(2,1)} fusion(s32[512]{0:T(512)S(1)} %compare_select_fusion.1, bf16[512,896]{1,0:T(8,128)(2,1)} %param.8, bf16[]{:T(256)} %constant.73.clone.1), kind=kCustom, calls=%fused_computation.62 | custom fusion | bytes 918016 | tf_op jit(solution)/shard_map/scatter | solution.py:59
  34.9 5.1 %all-to-all-done = s32[64,1,8]{2,1,0:T(1,128)S(1)} async-done(((s32[64,1,8]{2,1,0:T(1,128)}), s32[64,1,8]{2,1,0:T(1,128)S(1)}, u32[]{:S(2)}, u32[]{:S(2)}) %all-to-all-start) | async-done | bytes 2080 | tf_op jit(solution)/shard_map/all_to_all | solution.py:149
  40.0 5.2 %all-to-all-start.1 = ((bf16[64,8,896]{2,1,0:T(8,128)(2,1)}), bf16[64,8,896]{2,1,0:T(8,128)(2,1)S(1)}, u32[]{:S(2)}, u32[]{:S(2)}) async-start(bf16[64,8,896]{2,1,0:T(8,128)(2,1)} %bitcast.6), calls=%async_computation.1 | async-start | bytes 1835008 | tf_op jit(solution)/shard_map/all_to_all | solution.py:148
  46.5 24.8 %all-to-all-done.1 = bf16[64,8,896]{2,1,0:T(8,128)(2,1)S(1)} async-done(((bf16[64,8,896]{2,1,0:T(8,128)(2,1)}), bf16[64,8,896]{2,1,0:T(8,128)(2,1)S(1)}, u32[]{:S(2)}, u32[]{:S(2)}) %all-to-all-start.1) | async-done | bytes 917536 | tf_op jit(solution)/shard_map/all_to_all | solution.py:148
  71.3 2.9 %scatter_custom_fusion.2 = bf16[512,896]{1,0:T(8,128)(2,1)S(1)} fusion(s32[512]{0:T(512)S(1)} %bitcast.108, bf16[64,8,896]{2,1,0:T(8,128)(2,1)S(1)} %all-to-all-done.1, bf16[]{:T(256)} %constant.73.clone.1), kind=kCustom, calls=%fused_computation.46 | custom fusion | bytes 1835010 | tf_op jit(solution)/shard_map/scatter | solution.py:59
  74.3 1.6 collective-permute-start
  75.9 2.0 collective-permute-done
  79.3 1.5 collective-permute-start.2
  81.7 39.0 %collective-permute-done.1 = bf16[1024,896]{1,0:T(8,128)(2,1)} collective-permute-done((bf16[1024,896]{1,0:T(8,128)(2,1)S(1)}, bf16[1024,896]{1,0:T(8,128)(2,1)}, u32[]{:S(2)}, u32[]{:S(2)}) %collective-permute-start.1) | collective-permute-done | bytes 1835040 | tf_op jit(solution)/shard_map/ppermute | solution.py:167
  122.0 2.0 fusion.53
  128.0 2.7 %fusion.38 = (f32[1024,64]{1,0:T(8,128)S(1)}, f32[1024,64]{1,0:T(8,128)}) fusion(f32[64]{0:T(128)S(1)} %multiply_exponential_fusion), kind=kLoop, calls=%fused_computation.60 | loop fusion | flops 65536 | bytes 524544 | tf_op jit(solution)/shard_map/cos | solution.py:39
  131.4 1.8 constant_dynamic-update-slice_fusion.4
  133.2 1.8 constant_dynamic-update-slice_fusion.3
  135.1 27.5 %collective-permute-done.3 = bf16[1024,896]{1,0:T(8,128)(2,1)} collective-permute-done((bf16[1024,896]{1,0:T(8,128)(2,1)}, bf16[1024,896]{1,0:T(8,128)(2,1)}, u32[]{:S(2)}, u32[]{:S(2)}) %collective-permute-start.3) | collective-permute-done | bytes 1835040 | tf_op jit(solution)/shard_map/ppermute | solution.py:167
  162.5 1.8 constant_dynamic-update-slice_fusion.2
  164.4 3.0 %copy-done.1 = bf16[1024,3584]{1,0:T(8,128)(2,1)} copy-done((bf16[1024,3584]{1,0:T(8,128)(2,1)}, bf16[1024,3584]{1,0:T(8,128)(2,1)S(1)}, u32[]{:S(2)}) %copy-start.1) | copy-done | bytes 7340056
  167.3 1.5 fusion
  168.9 15.6 %broadcast_select_fusion = (bf16[1024,1152]{1,0:T(8,128)(2,1)}, bf16[1024,1152]{1,0:T(8,128)(2,1)S(1)}) fusion(pred[1024]{0:T(1024)(128)(4,1)S(1)} %copy-done.7, f32[1152]{0:T(1024)S(1)} %convert_element_type.67, bf16[3584,1152]{1,0:T(8,128)(2,1)} %all-gather.2.cloned.1.call-done, bf16[1024,3584]{1,0:T(8,128)(2,1)} %copy-done.1, ...), kind=kOutput, calls=%fused_computation.31 | convolution fusion | flops 8473935872 | bytes 20340224 | tf_op jit(solution)/shard_map/dot_general | solution.py:179
  184.6 6.3 %dynamic_update_slice.19 = bf16[1024,1152]{1,0:T(8,128)(2,1)} dynamic-update-slice(bf16[1024,1152]{1,0:T(8,128)(2,1)} %get-tuple-element.18, bf16[512,1152]{1,0:T(8,128)(2,1)S(1)} %slice.64, s32[]{:T(128)S(6)} %select_n.97, s32[]{:T(128)} %constant.69.clone.1) | dynamic-update-slice | bytes 2359300 | tf_op jit(solution)/shard_map/dynamic_update_slice | solution.py:64
  191.9 3.6 %slice_convert_fusion = f32[1024,896]{1,0:T(8,128)} fusion(bf16[1024,1152]{1,0:T(8,128)(2,1)} %dynamic_update_slice.19), kind=kLoop, calls=%fused_computation.34 | loop fusion | flops 917504 | bytes 5505024 | tf_op jit(solution)/shard_map/convert_element_type | solution.py:45
  195.7 5.1 %copy.47 = f32[1024,896]{0,1:T(8,128)} copy(f32[1024,896]{1,0:T(8,128)} %slice_convert_fusion) | data formatting | bytes 7340032 | tf_op jit(solution)/shard_map/convert_element_type | solution.py:45
  200.7 5.0 %copy.48 = f32[1024,7,128]{2,0,1:T(8,128)} copy(f32[1024,7,128]{0,2,1:T(8,128)} %bitcast.104) | data formatting | bytes 7340032 | tf_op jit(solution)/shard_map/convert_element_type | solution.py:45
  205.8 4.4 %slice_negate_fusion = (f32[1024,7,64]{2,0,1:T(8,128)S(1)}, f32[1024,7,64]{2,0,1:T(8,128)S(1)}) fusion(f32[1024,7,128]{2,0,1:T(8,128)} %copy.48), kind=kLoop, calls=%fused_computation.24 | loop fusion | flops 458752 | bytes 7340032 | tf_op jit(solution)/shard_map/neg | solution.py:47
  210.2 1.6 fusion.35
  214.7 1.5 fusion.11
  216.2 4.0 %fusion.22 = bf16[1,128,7,512]{3,1,2,0:T(8,128)(2,1)} fusion(f32[7,512]{1,0:T(8,128)S(1)} %fusion.11, f32[7,512]{1,0:T(8,128)S(1)} %get-tuple-element.22, f32[512,512,7]{1,0,2:T(8,128)S(1)} %get-tuple-element.23, pred[512,512]{0,1:T(8,128)(4,1)S(1)} %fusion.27, pred[512]{0:T(512)(128)(4,1)S(1)} %get-tuple-element.24, ...), kind=kOutput, calls=%fused_computation.39 | convolution fusion | flops 479854592 | bytes 8679936 | tf_op jit(solution)/shard_map/kgqs,skd->qkgd/dot_general | solution.py:105
  220.3 1.5 copy.55
  221.8 6.5 %fusion.4 = (f32[7,512]{1,0:T(8,128)S(1)}, f32[1024,512,7]{1,0,2:T(8,128)}) fusion(pred[512,1024]{0,1:T(8,128)(4,1)S(1)} %fusion.20, bf16[1024,7,128]{2,0,1:T(8,128)(2,1)S(1)} %fusion.16, bf16[1024,128]{1,0:T(8,128)(2,1)S(1)} %get-tuple-element.9), kind=kOutput, calls=%fused_computation.12 | convolution fusion | flops 950530560 | bytes 16398336 | tf_op jit(solution)/shard_map/qkgd,skd->kgqs/dot_general | solution.py:90
  228.4 8.2 %fusion.3 = f32[7,512]{1,0:T(8,128)S(1)} fusion(f32[1024,512,7]{1,0,2:T(8,128)} %get-tuple-element.21, f32[7,512]{1,0:T(8,128)S(1)} %get-tuple-element.20, pred[512,1024]{0,1:T(8,128)(4,1)S(1)} %fusion.20), kind=kLoop, calls=%fused_computation.11 | loop fusion | flops 14676480 | bytes 15233024 | tf_op jit(solution)/shard_map/reduce_sum | solution.py:104
  236.5 7.9 %fusion.21 = bf16[1,128,7,512]{3,1,2,0:T(8,128)(2,1)S(1)} fusion(f32[7,512]{1,0:T(8,128)S(1)} %fusion.3, f32[7,512]{1,0:T(8,128)S(1)} %get-tuple-element.20, f32[1024,512,7]{1,0,2:T(8,128)} %get-tuple-element.21, pred[512,1024]{0,1:T(8,128)(4,1)S(1)} %fusion.20, pred[512]{0:T(512)(128)(4,1)S(1)} %get-tuple-element.25, ...), kind=kOutput, calls=%fused_computation.37 | convolution fusion | flops 958791680 | bytes 16413184 | tf_op jit(solution)/shard_map/kgqs,skd->qkgd/dot_general | solution.py:105
  (66 shorter events, 20.6 us)
Async XLA Ops:
  6.5 162.3 %all-gather.2.cloned.1.call-start = ((), (), s32[]{:S(2)}) async-start(), calls=%async_computation.2 | async-start | bytes 8386560 | tf_op jit(solution)/shard_map/all_gather | solution.py:178
  7.3 73.8 %copy-start.3 = (bf16[3584]{0:T(1024)(128)(2,1)S(1)}, bf16[3584]{0:T(1024)(128)(2,1)}, u32[]{:S(2)}) copy-start(bf16[3584]{0:T(1024)(128)(2,1)} %param.13) | copy-start | bytes 21508
  7.9 73.1 %copy-start.4 = (bf16[1152]{0:T(1024)(128)(2,1)S(1)}, bf16[1152]{0:T(1024)(128)(2,1)}, u32[]{:S(2)}) copy-start(bf16[1152]{0:T(1024)(128)(2,1)} %param.15) | copy-start | bytes 6916
  8.0 112.7 %copy-start.6 = (s32[64]{0:T(128)S(1)}, s32[64]{0:T(128)}, u32[]{:S(2)}) copy-start(s32[64]{0:T(128)} %param.12) | copy-start | bytes 772
  8.0 114.0 %copy-start.5 = (s32[64]{0:T(128)S(1)}, s32[64]{0:T(128)}, u32[]{:S(2)}) copy-start(s32[64]{0:T(128)} %param.11) | copy-start | bytes 772
  17.5 22.5 %all-to-all-start = ((s32[64,1,8]{2,1,0:T(1,128)}), s32[64,1,8]{2,1,0:T(1,128)S(1)}, u32[]{:S(2)}, u32[]{:S(2)}) async-start(s32[64,1,8]{2,1,0:T(1,128)} %bitcast.4), calls=%async_computation | async-start | bytes 65536 | tf_op jit(solution)/shard_map/all_to_all | solution.py:149
  40.0 31.3 %all-to-all-start.1 = ((bf16[64,8,896]{2,1,0:T(8,128)(2,1)}), bf16[64,8,896]{2,1,0:T(8,128)(2,1)S(1)}, u32[]{:S(2)}, u32[]{:S(2)}) async-start(bf16[64,8,896]{2,1,0:T(8,128)(2,1)} %bitcast.6), calls=%async_computation.1 | async-start | bytes 1835008 | tf_op jit(solution)/shard_map/all_to_all | solution.py:148
  74.3 3.7 %collective-permute-start = (bf16[512,896]{1,0:T(8,128)(2,1)S(1)}, bf16[512,896]{1,0:T(8,128)(2,1)S(1)}, u32[]{:S(2)}, u32[]{:S(2)}) collective-permute-start(bf16[512,896]{1,0:T(8,128)(2,1)S(1)} %scatter_custom_fusion.2), channel_id=1, source_target_pairs={{0,4},{4,0},{8,12},{12,8},{16,20},{20,16},{24,28},{28,24},{32,36},... | collective-permute-start | bytes 2752520 | tf_op jit(solution)/shard_map/ppermute | solution.py:18
  78.1 42.6 %collective-permute-start.1 = (bf16[1024,896]{1,0:T(8,128)(2,1)S(1)}, bf16[1024,896]{1,0:T(8,128)(2,1)}, u32[]{:S(2)}, u32[]{:S(2)}) collective-permute-start(bf16[1024,896]{1,0:T(8,128)(2,1)S(1)} %constant_dynamic-update-slice_fusion), channel_id=1, source_target_pairs={{0,1},{1,2},{2,3},{3,0},{4,5},{5,6},{6,7},{7,4},{8,9},{9,10},{10,1... | collective-permute-start | bytes 5505032 | tf_op jit(solution)/shard_map/ppermute | solution.py:167
  79.3 53.9 %collective-permute-start.2 = (bf16[1024,896]{1,0:T(8,128)(2,1)S(1)}, bf16[1024,896]{1,0:T(8,128)(2,1)}, u32[]{:S(2)}, u32[]{:S(2)}) collective-permute-start(bf16[1024,896]{1,0:T(8,128)(2,1)S(1)} %constant_dynamic-update-slice_fusion), channel_id=1, source_target_pairs={{0,3},{1,0},{2,1},{3,2},{4,7},{5,4},{6,5},{7,6},{8,11},{9,8},{10,9... | collective-permute-start | bytes 5505032 | tf_op jit(solution)/shard_map/ppermute | solution.py:172
  120.7 41.8 %collective-permute-start.3 = (bf16[1024,896]{1,0:T(8,128)(2,1)}, bf16[1024,896]{1,0:T(8,128)(2,1)}, u32[]{:S(2)}, u32[]{:S(2)}) collective-permute-start(bf16[1024,896]{1,0:T(8,128)(2,1)} %collective-permute-done.1), channel_id=1, source_target_pairs={{0,1},{1,2},{2,3},{3,0},{4,5},{5,6},{6,7},{7,4},{8,9},{9,10},{10,1... | collective-permute-start | bytes 5505032 | tf_op jit(solution)/shard_map/ppermute | solution.py:167
  135.0 33.8 %copy-start.7 = (pred[1024]{0:T(1024)(128)(4,1)S(1)}, pred[1024]{0:T(1024)(128)(4,1)}, u32[]{:S(2)}) copy-start(pred[1024]{0:T(1024)(128)(4,1)} %constant.72.clone.1) | copy-start | bytes 3076
  164.3 3.0 %copy-start.1 = (bf16[1024,3584]{1,0:T(8,128)(2,1)}, bf16[1024,3584]{1,0:T(8,128)(2,1)S(1)}, u32[]{:S(2)}) copy-start(bf16[1024,3584]{1,0:T(8,128)(2,1)S(1)} %constant_dynamic-update-slice_fusion.2) | copy-start | bytes 22020100
  205.8 4.4 %copy-start.2 = (f32[1024,64]{1,0:T(8,128)S(1)}, f32[1024,64]{1,0:T(8,128)}, u32[]{:S(2)}) copy-start(f32[1024,64]{1,0:T(8,128)} %get-tuple-element.15) | copy-start | bytes 786436
  210.2 2.1 copy-start
Sparse Core Ops, SparseCore 0:
  10.0 89.1 all-gather.1
